TPU v7x, 256 devices: a whole 4x4x8 slice. The times are simulated.
256 devices in a mesh: seq: 16 (over z, y_lo), res: 16 (over y_hi, x, core).
Axes of the slice: x: 4, y: 4 (y_hi: 2, y_lo: 2; y = y_hi * 2 + y_lo), z: 8, core: 2. Of those that a mesh axis runs over, the one named last changes fastest.
Arguments:
- target_alignment_matrix: float32 [1024, 128, 256], P('seq', 'res'), may hold values from -6 to 6
- source_alignment_matrix: float32 [1024, 128, 256], P('seq', 'res'), may hold values from -6 to 6
- source_mapping_matrix: float32 [256, 32], replicated, may hold values from -0.375 to 0.375
- target_mapping_matrix: float32 [256, 32], replicated, may hold values from -0.375 to 0.375
- final_mapping_matrix: float32 [1024, 128], replicated, may hold values from -6 to 6
- edge_offset_vector: float32 [128], replicated, may hold values from -3 to 3
- edge_delta_cotangent: float32 [128, 128, 128], P('seq', 'res'), may hold values from -6 to 6
Outputs:
- edge_delta_result: float32 [128, 128, 128], P('seq', 'res')
- grad_cols: float32 [1024, 128, 256], P('seq', 'res')
- grad_rows: float32 [1024, 128, 256], P('seq', 'res')
- grad_left: float32 [256, 32], replicated
- grad_right: float32 [256, 32], replicated
- grad_proj: float32 [1024, 128], replicated
- grad_bias: float32 [128], replicated
All inputs are finite; a program needn't handle non-finite values.
Results may differ from a plain program's by a relative error of at most 0.00013.
Values sent between devices are 32-bit elements; how exact they have to be, the bound alone decides.
A program may use at most 64 MiB of HBM per device.

v0:
```python
import jax
import jax.numpy as jnp
from jax import lax
from jax.sharding import PartitionSpec as P


def standardize_features(values):
    average = jnp.mean(values, axis=-1, keepdims=True)
    centred = values - average
    inverse = lax.rsqrt(jnp.mean(centred * centred, axis=-1, keepdims=True) + 1e-05)
    return (centred * inverse, inverse)


def normalize_back(normed, inverse, upstream):
    first = jnp.mean(upstream, axis=-1, keepdims=True)
    second = jnp.mean(upstream * normed, axis=-1, keepdims=True)
    return inverse * (upstream - first - normed * second)


def body(
    target_alignment_matrix,
    source_alignment_matrix,
    source_mapping_matrix,
    target_mapping_matrix,
    final_mapping_matrix,
    edge_offset_vector,
    edge_delta_cotangent,
):
    exact_arithmetic = lax.Precision.HIGHEST
    member_tally, amino_tally, feature_tally = target_alignment_matrix.shape
    hidden = source_mapping_matrix.shape[1]
    square = hidden * hidden
    pair_width = final_mapping_matrix.shape[1]
    seqs_total = member_tally * lax.axis_size("seq")
    own_rows = edge_delta_cotangent.shape[0]
    source_scaling_divisor, source_inverted_scale = standardize_features(source_alignment_matrix)
    target_scaling_divisor, target_inverted_scale = standardize_features(target_alignment_matrix)
    left_rows = jnp.einsum(
        "uwh,hq->uwq", source_scaling_divisor, source_mapping_matrix, precision=exact_arithmetic
    )
    right_cols = jnp.einsum(
        "iwe,ed->iwd", target_scaling_divisor, target_mapping_matrix, precision=exact_arithmetic
    )
    left_full = lax.all_gather(left_rows, "res", axis=1, tiled=True)
    slab_rows = left_full.shape[1]
    partial_value = (
        jnp.einsum("ipu,ihl->phul", left_full, right_cols, precision=exact_arithmetic) / seqs_total
    )
    partial_value = partial_value.reshape(slab_rows, amino_tally, square)
    flat_grad = edge_delta_cotangent.reshape(own_rows * amino_tally, pair_width)
    reduced = lax.psum_scatter(partial_value, "seq", scatter_dimension=0, tiled=True)
    reduced_flat = reduced.reshape(own_rows * amino_tally, square)
    edge_delta_result = (
        jnp.dot(reduced_flat, final_mapping_matrix, precision=exact_arithmetic).reshape(
            own_rows, amino_tally, pair_width
        )
        + edge_offset_vector
    )
    local_grad = jnp.dot(flat_grad, final_mapping_matrix.T, precision=exact_arithmetic).reshape(
        own_rows, amino_tally, square
    )
    grad_full = lax.all_gather(local_grad, "seq", axis=0, tiled=True)
    grad_out = jnp.einsum("pa,pb->ab", reduced_flat, flat_grad, precision=exact_arithmetic)
    grad_four = grad_full.reshape(slab_rows, amino_tally, hidden, hidden)
    grad_left_part = (
        jnp.einsum("ijhk,sjk->sih", grad_four, right_cols, precision=exact_arithmetic) / seqs_total
    )
    grad_right_side = (
        jnp.einsum("ijhk,sih->sjk", grad_four, left_full, precision=exact_arithmetic) / seqs_total
    )
    grad_left_side = lax.psum_scatter(grad_left_part, "res", scatter_dimension=1, tiled=True)
    grad_wleft = jnp.einsum(
        "sic,sih->ch", source_scaling_divisor, grad_left_side, precision=exact_arithmetic
    )
    grad_wright = jnp.einsum(
        "sjc,sjh->ch", target_scaling_divisor, grad_right_side, precision=exact_arithmetic
    )
    grad_bpart = jnp.sum(flat_grad, axis=0)
    grad_left, grad_right, grad_proj, grad_bias = lax.psum(
        (grad_wleft, grad_wright, grad_out, grad_bpart), ("seq", "res")
    )
    upstream_rows = jnp.einsum(
        "sih,ch->sic", grad_left_side, source_mapping_matrix, precision=exact_arithmetic
    )
    upstream_cols = jnp.einsum(
        "sjh,ch->sjc", grad_right_side, target_mapping_matrix, precision=exact_arithmetic
    )
    grad_rows = normalize_back(source_scaling_divisor, source_inverted_scale, upstream_rows)
    grad_cols = normalize_back(target_scaling_divisor, target_inverted_scale, upstream_cols)
    return (edge_delta_result, grad_cols, grad_rows, grad_left, grad_right, grad_proj, grad_bias)


def solution(mesh):
    in_specs = (
        P("seq", "res", None),
        P("seq", "res", None),
        P(),
        P(),
        P(),
        P(),
        P("seq", "res", None),
    )
    out_specs = (
        P("seq", "res", None),
        P("seq", "res", None),
        P("seq", "res", None),
        P(),
        P(),
        P(),
        P(),
    )
    return jax.shard_map(body, mesh=mesh, in_specs=in_specs, out_specs=out_specs, check_vma=False)
```

profile of v0, /device:TPU:2, one launch (start us, length us, event | category | flops | bytes accessed | tf_op | source)
XLA Modules:
  0.0 883.1 jit_solution(16809121184989202640)
XLA Ops:
  7.3 1.0 copy-done
  8.2 2.1 fusion.9
  10.4 1.2 reduce_sum.83
  11.6 1.3 multiply_reduce_fusion.2
  12.9 2.4 fusion.13
  15.4 1.2 reduce_sum.81
  17.6 95.0 %all-gather.5.cloned.1.call-done = f32[128,8,1024]{2,1,0:T(8,128)} async-done(((f32[8,8,1024]{2,1,0:T(8,128)}), f32[128,8,1024]{2,1,0:T(8,128)}) %all-gather.5.cloned.1.call-update) | async-done | bytes 4194320 | tf_op jit(solution)/shard_map/all_gather | solution.py:62
  112.6 5.4 copy.41
  118.0 10.2 %bitcast_multiply_fusion = f32[64,128,32]{0,1,2:T(8,128)} fusion(f32[128,8,32,32]{0,3,2,1:T(8,128)} %bitcast.65, f32[64,8,32]{0,2,1:T(8,128)S(1)} %copy.44), kind=kOutput, calls=%fused_computation.1 | convolution fusion | flops 805568512 | bytes 5308416 | tf_op jit(solution)/shard_map/ijhk,sjk->sih/dot_general | solution.py:66
  128.5 50.5 %all-gather.3.cloned.1.call-done = f32[64,128,32]{2,1,0:T(8,128)} async-done(((f32[64,8,32]{2,1,0:T(8,128)}), f32[64,128,32]{2,1,0:T(8,128)}) %all-gather.3.cloned.1.call-update) | async-done | bytes 1048592 | tf_op jit(solution)/shard_map/all_gather | solution.py:44
  179.0 4.4 copy.39
  183.4 8.2 convolution_multiply_fusion
  191.6 5.6 copy.40
  197.2 0.7 copy-done.3
  198.4 6.8 fusion.6
  205.4 1.4 convolution_bitcast_fusion.1
  206.8 0.6 fusion.31
  207.4 1.1 subtract_multiply_fusion.1
  208.6 52.0 %reduce-scatter.5.cloned.1.call-done = f32[64,8,32]{0,1,2:T(8,128)} async-done(((f32[64,128,32]{0,1,2:T(8,128)}), f32[64,8,32]{0,1,2:T(8,128)}) %reduce-scatter.5.cloned.1.call-update) | async-done | bytes 65552 | tf_op jit(solution)/shard_map/reduce_scatter | solution.py:71
  260.6 1.1 copy.46
  261.7 1.4 convolution_bitcast_fusion.2
  263.0 0.6 fusion.30
  263.8 99.2 %reduce-scatter.3.cloned.1.call-done = f32[8,8,1024]{2,1,0:T(8,128)} async-done(((f32[128,8,1024]{2,1,0:T(8,128)}), f32[8,8,1024]{2,1,0:T(8,128)}) %reduce-scatter.3.cloned.1.call-update) | async-done | bytes 262160 | tf_op jit(solution)/shard_map/reduce_scatter | solution.py:51
  363.0 2.7 convolution_bitcast_fusion
  365.8 1.1 subtract_multiply_fusion
  366.9 2.0 convolution_add_fusion
  368.9 243.2 %all-reduce.6.cloned.1.call-done = (f32[256,32]{0,1:T(8,128)}, f32[256,32]{0,1:T(8,128)}, f32[128]{0:T(128)}) async-done(((f32[256,32]{0,1:T(8,128)}, f32[256,32]{0,1:T(8,128)}, f32[128]{0:T(128)}), (f32[256,32]{0,1:T(8,128)}, f32[256,32]{0,1:T(8,128)}, f32[128]{0:T(128)})) %all-reduce.6.cloned.1.call-update) | async-done | bytes 66064 | tf_op jit(solution)/shard_map/psum | solution.py:79
  612.1 258.4 %all-reduce.4.cloned.1.call-done = f32[1024,128]{1,0:T(8,128)} async-done(((f32[1024,128]{1,0:T(8,128)}), f32[1024,128]{1,0:T(8,128)}) %all-reduce.4.cloned.1.call-update) | async-done | bytes 524304 | tf_op jit(solution)/shard_map/psum | solution.py:79
  870.5 1.4 copy.60
  871.9 1.4 copy.61
  873.3 1.9 copy.62
  875.1 1.1 copy.63
  (37 shorter events, 2.3 us)
Async XLA Ops:
  7.2 1.0 copy-start
  7.2 9.4 %copy-start.1 = (f32[64,8,256]{2,1,0:T(8,128)S(1)}, f32[64,8,256]{2,1,0:T(8,128)}, u32[]{:S(2)}) copy-start(f32[64,8,256]{2,1,0:T(8,128)} %param.7) | copy-start | bytes 1572868
  7.2 9.6 %copy-start.4 = (f32[256,32]{0,1:T(8,128)S(1)}, f32[256,32]{0,1:T(8,128)}, u32[]{:S(2)}) copy-start(f32[256,32]{0,1:T(8,128)} %param.10) | copy-start | bytes 98308
  7.2 105.4 %all-gather.5.cloned.1.call-start = ((), (), s32[]{:S(2)}) async-start(), calls=%async_computation.4 | async-start | bytes 4456448 | tf_op jit(solution)/shard_map/all_gather | solution.py:62
  10.4 168.6 %all-gather.3.cloned.1.call-start = ((), (), s32[]{:S(2)}) async-start(), calls=%async_computation.2 | async-start | bytes 4456448 | tf_op jit(solution)/shard_map/all_gather | solution.py:44
  15.3 245.3 %reduce-scatter.5.cloned.1.call-start = ((), (), s32[]{:S(2)}) async-start(), calls=%async_computation.5 | async-start | bytes 2228224 | tf_op jit(solution)/shard_map/reduce_scatter | solution.py:71
  128.3 234.7 %reduce-scatter.3.cloned.1.call-start = ((), (), s32[]{:S(2)}) async-start(), calls=%async_computation.3 | async-start | bytes 4456448 | tf_op jit(solution)/shard_map/reduce_scatter | solution.py:51
  197.2 0.8 copy-start.3
  197.2 9.6 %copy-start.5 = (f32[256,32]{0,1:T(8,128)S(1)}, f32[256,32]{0,1:T(8,128)}, u32[]{:S(2)}) copy-start(f32[256,32]{0,1:T(8,128)} %param.10) | copy-start | bytes 98308
  197.2 414.9 %all-reduce.6.cloned.1.call-start = ((), (), s32[]{:S(2)}) async-start(), calls=%async_computation.7 | async-start | bytes 132096 | tf_op jit(solution)/shard_map/psum | solution.py:79
  205.2 56.5 %copy-start.2 = (f32[64,8,256]{2,1,0:T(8,128)S(1)}, f32[64,8,256]{2,1,0:T(8,128)}, u32[]{:S(2)}) copy-start(f32[64,8,256]{2,1,0:T(8,128)} %param.8) | copy-start | bytes 1572868
  205.2 57.8 %copy-start.6 = (f32[256,32]{0,1:T(8,128)S(1)}, f32[256,32]{0,1:T(8,128)}, u32[]{:S(2)}) copy-start(f32[256,32]{0,1:T(8,128)} %param.9) | copy-start | bytes 98308
  207.4 159.5 %copy-start.7 = (f32[128]{0:T(128)S(1)}, f32[128]{0:T(128)}, u32[]{:S(2)}) copy-start(f32[128]{0:T(128)} %param.12) | copy-start | bytes 1540
  263.7 606.8 %all-reduce.4.cloned.1.call-start = ((), (), s32[]{:S(2)}) async-start(), calls=%async_computation.6 | async-start | bytes 1048576 | tf_op jit(solution)/shard_map/psum | solution.py:79
Sparse Core Ops, SparseCore 0:
  10.5 102.0 all-gather.4
  115.7 63.2 all-gather.2
  183.3 77.3 reduce-scatter.4
  263.0 99.9 reduce-scatter.2
  369.5 242.5 all-reduce.5
  618.0 252.4 all-reduce.3
where the time goes:
time: 884 us; the launch traced here: 883 us
  waiting for transfers between devices  798 us (90%)
  matrix products  39.1 us (4%)
  local copies, waits for them, and re-layouts  24.1 us (3%)
  between operations  14.3 us (2%)
    psum x2, waiting for transfers between devices, body(): lax.psum((grad_wleft, grad_wright, grad_out, grad_bpart), ('seq', 'res'))  502 us
    reduce_scatter x1, waiting for transfers between devices, body(): lax.psum_scatter(partial_value, 'seq', scatter_dimension=0, tiled=True)  99.2 us
    all_gather x1, waiting for transfers between devices, body(): grad_full = lax.all_gather(local_grad, 'seq', axis=0, tiled=True)  95 us
    reduce_scatter x1, waiting for transfers between devices, body(): lax.psum_scatter(grad_left_part, 'res', scatter_dimension=1, tiled=True)  52 us
    all_gather x1, waiting for transfers between devices, body(): left_full = lax.all_gather(left_rows, 'res', axis=1, tiled=True)  50.5 us
  transfers between devices with their start and end apart: 6, of which 6 were waited for; matrix products, arithmetic and copies ran while one was open for 7% of the time, Pallas kernels for 0%

commit v1 on v0

--- a/solution.py
+++ b/solution.py
@@ -59,7 +59,9 @@
     local_grad = jnp.dot(flat_grad, final_mapping_matrix.T, precision=exact_arithmetic).reshape(
         own_rows, amino_tally, square
     )
-    grad_full = lax.all_gather(local_grad, "seq", axis=0, tiled=True)
+    grad_full = jnp.concatenate(
+        lax.all_to_all(jnp.stack([local_grad] * lax.axis_size("seq")), "seq", 0, 0), axis=0
+    )
     grad_out = jnp.einsum("pa,pb->ab", reduced_flat, flat_grad, precision=exact_arithmetic)
     grad_four = grad_full.reshape(slab_rows, amino_tally, hidden, hidden)
     grad_left_part = (

time: 884 us -> 874 us (0.989)
  waiting for transfers between devices: 798 us -> 690 us
  matrix products: 39.1 us -> 98.6 us
  starting transfers between devices: 0.43 us -> 25.7 us
    all_gather x1 -> x0, waiting for transfers between devices: 95 us -> none  [body(): grad_full = lax.all_gather(local_grad, 'seq', axis=0, tiled=True)]
    all_to_all x0 -> x1, waiting for transfers between devices: none -> 94.4 us  [body(): lax.all_to_all(jnp.stack([local_grad] * lax.axis_size('seq')), 'seq', 0, 0)]
    reduce_scatter x1, waiting for transfers between devices: 52 us -> 0.01 us  [body(): lax.psum_scatter(grad_left_part, 'res', scatter_dimension=1, tiled=True)]
    all_gather x1, waiting for transfers between devices: 50.5 us -> 0.02 us  [body(): left_full = lax.all_gather(left_rows, 'res', axis=1, tiled=True)]
    dot_general x1, matrix products: 6.76 us -> 43.7 us  [body(): jnp.einsum('ijhk,sih->sjk', grad_four, left_full, precision=exact_arithme...]
    dot_general x1, matrix products: 10.2 us -> 34.6 us  [body(): jnp.einsum('ijhk,sjk->sih', grad_four, right_cols, precision=exact_arithm...]
    reduce_scatter x1, starting transfers between devices: 0.22 us -> 15.8 us  [body(): lax.psum_scatter(partial_value, 'seq', scatter_dimension=0, tiled=True)]
    another operation x0 -> x2, local copies, waits for them, and re-layouts: none -> 14.2 us  [the longest x1 11.7 us: body(): grad_four = grad_full.reshape(slab_rows, amino_tally, hidden, hidden)]
  transfers between devices with their start and end apart: 6 -> 6, of which waited for: 6 -> 4; matrix products, arithmetic and copies ran while one was open for 7% -> 14% of each run, Pallas kernels for 0% -> 0%
where the time goes in v1:
time: 874 us; the launch traced here: 865 us
  waiting for transfers between devices  690 us (79%)
  matrix products  98.6 us (11%)
  local copies, waits for them, and re-layouts  32.9 us (4%)
  starting transfers between devices  25.7 us (3%)
  between operations  14.4 us (2%)
    psum x2, waiting for transfers between devices, body(): lax.psum((grad_wleft, grad_wright, grad_out, grad_bpart), ('seq', 'res'))  501 us
    all_to_all x1, waiting for transfers between devices, body(): lax.all_to_all(jnp.stack([local_grad] * lax.axis_size('seq')), 'seq', 0, 0)  94.4 us
    reduce_scatter x1, waiting for transfers between devices, body(): lax.psum_scatter(partial_value, 'seq', scatter_dimension=0, tiled=True)  93.9 us
    dot_general x1, matrix products, body(): jnp.einsum('ijhk,sih->sjk', grad_four, left_full, precision=exact_arithme...  43.7 us
    dot_general x1, matrix products, body(): jnp.einsum('ijhk,sjk->sih', grad_four, right_cols, precision=exact_arithm...  34.6 us
  transfers between devices with their start and end apart: 6, of which 4 were waited for; matrix products, arithmetic and copies ran while one was open for 14% of the time, Pallas kernels for 0%

profile of v1, /device:TPU:2, one launch (start us, length us, event | category | flops | bytes accessed | tf_op | source)
XLA Modules:
  0.0 864.8 jit_solution(17547039853970959588)
XLA Ops:
  7.2 1.0 copy-done
  8.2 1.4 fusion.18
  9.6 2.5 stack.3
  12.1 9.8 %all-to-all-start = ((f32[16,8,8,1024]{3,2,1,0:T(8,128)}), f32[16,8,8,1024]{3,2,1,0:T(8,128)}, u32[]{:S(2)}, u32[]{:S(2)}) async-start(f32[16,8,8,1024]{3,2,1,0:T(8,128)} %stack.3), calls=%async_computation.1 | async-start | bytes 8388608 | tf_op jit(solution)/shard_map/all_to_all | solution.py:63
  22.4 1.3 fusion.22
  24.2 0.6 fusion.21
  25.0 94.4 %all-to-all-done = f32[16,8,8,1024]{3,2,1,0:T(8,128)} async-done(((f32[16,8,8,1024]{3,2,1,0:T(8,128)}), f32[16,8,8,1024]{3,2,1,0:T(8,128)}, u32[]{:S(2)}, u32[]{:S(2)}) %all-to-all-start) | async-done | bytes 4194336 | tf_op jit(solution)/shard_map/all_to_all | solution.py:63
  119.4 11.7 %reshape_reshape.3 = f32[128,8,32,32]{3,2,1,0:T(8,128)} reshape(f32[16,8,8,1024]{3,2,1,0:T(8,128)} %all-to-all-done) | data formatting | bytes 8388608 | tf_op jit(solution)/shard_map/reshape;reshape | solution.py:66
  131.1 34.6 %bitcast_multiply_fusion = f32[64,128,32]{0,1,2:T(8,128)} fusion(f32[128,8,32,32]{3,2,1,0:T(8,128)} %reshape_reshape.3, f32[64,8,32]{0,2,1:T(8,128)S(1)} %copy.32), kind=kOutput, calls=%fused_computation.5 | convolution fusion | flops 805568512 | bytes 5308416 | tf_op jit(solution)/shard_map/ijhk,sjk->sih/dot_general | solution.py:68
  165.6 15.8 %reduce-scatter.3.cloned.1.call-start = ((), (), s32[]{:S(2)}) async-start(), calls=%async_computation.4 | async-start | bytes 4456448 | tf_op jit(solution)/shard_map/reduce_scatter | solution.py:51
  181.4 4.4 copy.27
  185.9 8.2 convolution_multiply_fusion
  194.1 5.5 copy.28
  199.6 0.7 copy-done.4
  200.3 0.5 reduce_sum.89
  200.9 43.7 %fusion.13 = f32[64,8,32]{0,2,1:T(8,128)S(1)} fusion(f32[128,8,32,32]{3,2,1,0:T(8,128)} %reshape_reshape.3, f32[64,128,32]{0,1,2:T(8,128)S(1)} %copy.27), kind=kOutput, calls=%fused_computation.10 | convolution fusion | flops 805322752 | bytes 5308416 | tf_op jit(solution)/shard_map/ijhk,sih->sjk/dot_general | solution.py:71
  244.7 1.4 convolution_bitcast_fusion.1
  246.1 0.6 fusion.40
  246.7 1.1 subtract_multiply_fusion.1
  247.9 1.1 copy.34
  248.9 1.4 convolution_bitcast_fusion.2
  250.3 0.6 fusion.39
  251.0 93.9 %reduce-scatter.3.cloned.1.call-done = f32[8,8,1024]{2,1,0:T(8,128)} async-done(((f32[128,8,1024]{2,1,0:T(8,128)}), f32[8,8,1024]{2,1,0:T(8,128)}) %reduce-scatter.3.cloned.1.call-update) | async-done | bytes 262160 | tf_op jit(solution)/shard_map/reduce_scatter | solution.py:51
  344.9 2.7 convolution_bitcast_fusion
  347.7 1.1 subtract_multiply_fusion
  348.8 2.0 convolution_add_fusion
  350.8 242.9 %all-reduce.6.cloned.1.call-done = (f32[256,32]{0,1:T(8,128)}, f32[256,32]{0,1:T(8,128)}, f32[128]{0:T(128)}) async-done(((f32[256,32]{0,1:T(8,128)}, f32[256,32]{0,1:T(8,128)}, f32[128]{0:T(128)}), (f32[256,32]{0,1:T(8,128)}, f32[256,32]{0,1:T(8,128)}, f32[128]{0:T(128)})) %all-reduce.6.cloned.1.call-update) | async-done | bytes 66064 | tf_op jit(solution)/shard_map/psum | solution.py:81
  593.8 258.4 %all-reduce.4.cloned.1.call-done = f32[1024,128]{1,0:T(8,128)} async-done(((f32[1024,128]{1,0:T(8,128)}), f32[1024,128]{1,0:T(8,128)}) %all-reduce.4.cloned.1.call-update) | async-done | bytes 524304 | tf_op jit(solution)/shard_map/psum | solution.py:81
  852.2 1.4 copy.63
  853.5 1.4 copy.64
  854.9 1.9 copy.65
  856.8 1.1 copy.66
  (41 shorter events, 1.4 us)
Async XLA Ops:
  7.2 1.0 copy-start
  12.1 9.8 %copy-start.2 = (f32[64,8,256]{2,1,0:T(8,128)S(1)}, f32[64,8,256]{2,1,0:T(8,128)}, u32[]{:S(2)}) copy-start(f32[64,8,256]{2,1,0:T(8,128)} %param.8) | copy-start | bytes 1572868
  12.1 10.3 %copy-start.7 = (f32[256,32]{0,1:T(8,128)S(1)}, f32[256,32]{0,1:T(8,128)}, u32[]{:S(2)}) copy-start(f32[256,32]{0,1:T(8,128)} %param.9) | copy-start | bytes 98308
  12.1 11.7 %copy-start.1 = (f32[64,8,256]{2,1,0:T(8,128)S(1)}, f32[64,8,256]{2,1,0:T(8,128)}, u32[]{:S(2)}) copy-start(f32[64,8,256]{2,1,0:T(8,128)} %param.7) | copy-start | bytes 1572868
  12.1 12.1 %copy-start.5 = (f32[256,32]{0,1:T(8,128)S(1)}, f32[256,32]{0,1:T(8,128)}, u32[]{:S(2)}) copy-start(f32[256,32]{0,1:T(8,128)} %param.10) | copy-start | bytes 98308
  12.1 107.2 %all-to-all-start = ((f32[16,8,8,1024]{3,2,1,0:T(8,128)}), f32[16,8,8,1024]{3,2,1,0:T(8,128)}, u32[]{:S(2)}, u32[]{:S(2)}) async-start(f32[16,8,8,1024]{3,2,1,0:T(8,128)} %stack.3), calls=%async_computation.1 | async-start | bytes 8388608 | tf_op jit(solution)/shard_map/all_to_all | solution.py:63
  21.9 159.5 %all-gather.2.cloned.1.call-start = ((), (), s32[]{:S(2)}) async-start(), calls=%async_computation.3 | async-start | bytes 4456448 | tf_op jit(solution)/shard_map/all_gather | solution.py:44
  23.7 224.1 %reduce-scatter.5.cloned.1.call-start = ((), (), s32[]{:S(2)}) async-start(), calls=%async_computation.5 | async-start | bytes 2228224 | tf_op jit(solution)/shard_map/reduce_scatter | solution.py:73
  165.6 179.3 %reduce-scatter.3.cloned.1.call-start = ((), (), s32[]{:S(2)}) async-start(), calls=%async_computation.4 | async-start | bytes 4456448 | tf_op jit(solution)/shard_map/reduce_scatter | solution.py:51
  199.6 0.8 copy-start.4
  199.6 394.2 %all-reduce.6.cloned.1.call-start = ((), (), s32[]{:S(2)}) async-start(), calls=%async_computation.7 | async-start | bytes 132096 | tf_op jit(solution)/shard_map/psum | solution.py:81
  200.9 45.2 %copy-start.6 = (f32[256,32]{0,1:T(8,128)S(1)}, f32[256,32]{0,1:T(8,128)}, u32[]{:S(2)}) copy-start(f32[256,32]{0,1:T(8,128)} %param.10) | copy-start | bytes 98308
  244.5 4.4 copy-start.3
  244.5 5.8 copy-start.8
  246.7 102.1 %copy-start.9 = (f32[128]{0:T(128)S(1)}, f32[128]{0:T(128)}, u32[]{:S(2)}) copy-start(f32[128]{0:T(128)} %param.12) | copy-start | bytes 1540
  251.0 601.2 %all-reduce.4.cloned.1.call-start = ((), (), s32[]{:S(2)}) async-start(), calls=%async_computation.6 | async-start | bytes 1048576 | tf_op jit(solution)/shard_map/psum | solution.py:81
Sparse Core Ops, SparseCore 0:
  25.8 85.8 all-gather.1
  165.8 76.9 reduce-scatter.4
  245.3 99.5 reduce-scatter.2
  351.4 242.3 all-reduce.5
  599.6 252.4 all-reduce.3
